TPU v7x, 32 devices: a whole 2x2x4 slice. The times are simulated.
32 devices in a mesh: vel: 16 (over z, x, core), gx: 2 (over y).
Axes of the slice: x: 2, y: 2, z: 4, core: 2. Of those that a mesh axis runs over, the one named last changes fastest.
Arguments:
- distribution: float32 [4096, 8, 256], P('vel', 'gx'), as said below
Outputs:
- relaxed: float32 [4096, 8, 256], P('vel', 'gx')
Inputs may be any that keep to these rules, and one draw needn't show every extreme that they name: `distribution`: every entry is positive.
All inputs are finite; a program needn't handle non-finite values.
Results may differ from a plain program's by a relative error of at most 0.0003.
Values sent between devices are 32-bit elements; how exact they have to be, the bound alone decides.
A program may use at most 64 MiB of HBM per device.

v0:
```python
import math

import jax
import jax.numpy as jnp
from jax import lax
from jax.sharding import PartitionSpec as P

NV1 = 16
NZ = 16
COLLISIONS = 2


speed_limit = 4.0
time_step = 0.05
knudsen = 0.0125


def extended(value, sides, width):
    for axis, dim in sides:
        size, length = (lax.axis_size(axis), value.shape[dim])
        up = [(i, (i + 1) % size) for i in range(size)]
        down = [(j, i) for i, j in up]
        last = lax.slice_in_dim(value, length - width, length, axis=dim)
        leading = lax.slice_in_dim(value, 0, width, axis=dim)
        before = lax.ppermute(last, axis, up)
        after = lax.ppermute(leading, axis, down)
        value = jnp.concatenate([before, value, after], axis=dim)
    return value


def velocities(index):
    spacing = 2.0 * speed_limit / (NV1 - 1)
    first = index % NV1
    rest = index // NV1
    second = rest // NV1
    third = rest % NV1
    return [-speed_limit + spacing * part.astype(jnp.float32) for part in (first, second, third)]


def quad_weight():
    spacing = 2.0 * speed_limit / (NV1 - 1)
    return spacing**3 / (2.0 * math.pi) ** 1.5


def along_z(field, offset):
    zpos = jnp.arange(field.shape[-1], dtype=jnp.int32) % NZ
    main = jnp.roll(field, offset, -1)
    if offset > 0:
        other = jnp.roll(field, offset - NZ, -1)
        keep = zpos >= offset
    else:
        other = jnp.roll(field, offset + NZ, -1)
        keep = zpos < NZ + offset
    return jnp.where(keep, main, other)


def backward(field, minus_one, minus_two):
    return (3.0 * field - 4.0 * minus_one + minus_two) * 0.5


def forward(field, plus_one, plus_two):
    return (-3.0 * field + 4.0 * plus_one - plus_two) * 0.5


def upwind(field, comp, minus_one, minus_two, plus_one, plus_two):
    return jnp.where(
        comp > 0, backward(field, minus_one, minus_two), forward(field, plus_one, plus_two)
    )


def transverse(field, comp_y, comp_z):
    deriv_y = upwind(
        field,
        comp_y,
        jnp.roll(field, NZ, -1),
        jnp.roll(field, 2 * NZ, -1),
        jnp.roll(field, -NZ, -1),
        jnp.roll(field, -2 * NZ, -1),
    )
    deriv_z = upwind(
        field, comp_z, along_z(field, 1), along_z(field, 2), along_z(field, -1), along_z(field, -2)
    )
    return (deriv_y, deriv_z)


def along_x(field, comp_x):
    padded = extended(field, (("gx", 1),), 2)
    return upwind(field, comp_x, padded[:, 1:-3], padded[:, :-4], padded[:, 3:-1], padded[:, 4:])


def rate(field, comp_x, comp_y, comp_z):
    deriv_x = along_x(field, comp_x)
    deriv_y, deriv_z = transverse(field, comp_y, comp_z)
    return -(comp_x * deriv_x + comp_y * deriv_y + comp_z * deriv_z)


def advance(field, comp_x, comp_y, comp_z):
    first = field + time_step * rate(field, comp_x, comp_y, comp_z)
    second = 0.75 * field + 0.25 * (first + time_step * rate(first, comp_x, comp_y, comp_z))
    return field / 3.0 + 2.0 / 3.0 * (second + time_step * rate(second, comp_x, comp_y, comp_z))


def primitive(moments):
    rho = moments[0]
    vel_x = moments[1] / rho
    vel_y = moments[2] / rho
    vel_z = moments[3] / rho
    temp = (moments[4] / rho - (vel_x * vel_x + vel_y * vel_y + vel_z * vel_z)) / 3.0
    return jnp.stack([rho, vel_x, vel_y, vel_z, temp])


def maxwell(prims, comp_x, comp_y, comp_z):
    spread = (comp_x - prims[1]) ** 2 + (comp_y - prims[2]) ** 2 + (comp_z - prims[3]) ** 2
    return prims[0] * prims[4] ** (-1.5) * jnp.exp(-spread / (2.0 * prims[4]))


def separable_mass(prims):
    spacing = 2.0 * speed_limit / (NV1 - 1)
    points = -speed_limit + spacing * jnp.arange(NV1, dtype=jnp.float32)
    product = quad_weight() * prims[0] * prims[4] ** (-1.5)
    for which in (1, 2, 3):
        offset = points[:, None] - prims[which][None, :]
        product = product * jnp.sum(jnp.exp(-(offset * offset) / (2.0 * prims[4])), 0)
    return product


def collide(field, comp_x, comp_y, comp_z):
    count = field.shape[0]
    flat = field.reshape(count, -1)
    ones = jnp.ones_like(comp_x)
    table = (
        jnp.stack(
            [ones, comp_x, comp_y, comp_z, comp_x * comp_x + comp_y * comp_y + comp_z * comp_z]
        )
        * quad_weight()
    )
    local = jnp.dot(table, flat, precision=lax.Precision.HIGHEST)
    prims = primitive(lax.psum(local, "vel"))
    dense = maxwell(prims, comp_x[:, None], comp_y[:, None], comp_z[:, None])
    mass = separable_mass(prims)
    scale = prims[0] / mass
    rates = time_step * prims[0] * jnp.sqrt(prims[4]) / knudsen
    return ((flat + rates * (dense * scale)) / (1.0 + rates)).reshape(field.shape)


def on_device(distribution):
    count = distribution.shape[0]
    index = lax.axis_index("vel") * count + jnp.arange(count, dtype=jnp.int32)
    comp_x, comp_y, comp_z = velocities(index)
    field = distribution
    for step in range(COLLISIONS):
        field = advance(field, comp_x[:, None, None], comp_y[:, None, None], comp_z[:, None, None])
        field = collide(field, comp_x, comp_y, comp_z)
    return field


def solution(mesh):
    return jax.shard_map(
        on_device,
        mesh=mesh,
        in_specs=(P("vel", "gx", None),),
        out_specs=P("vel", "gx", None),
        check_vma=False,
    )
```

profile of v0, /device:TPU:0, one launch (start us, length us, event | category | flops | bytes accessed | tf_op | source)
XLA Modules:
  0.0 386.0 jit_solution(4824331936601160539)
XLA Ops:
  0.0 2.1 fusion.320
  2.9 3.0 collective-permute-start.1
  13.6 1.5 fusion.316
  15.1 1.5 fusion.318
  16.5 1.5 fusion.313
  18.0 1.5 fusion.309
  21.3 1.5 fusion.310
  22.8 2.1 copy.101
  24.8 4.6 %collective-permute-done = f32[256,2,256]{2,0,1:T(8,128)} collective-permute-done((f32[256,2,256]{2,0,1:T(8,128)}, f32[256,2,256]{2,0,1:T(8,128)}, u32[]{:S(2)}, u32[]{:S(2)}) %collective-permute-start) | collective-permute-done | bytes 524320 | tf_op jit(solution)/shard_map/ppermute | solution.py:25
  29.4 2.0 copy.96
  31.4 7.4 %fusion.104 = f32[256,4,256]{0,2,1:T(8,128)S(1)} fusion(f32[256,4,256]{0,2,1:T(8,128)S(1)} %copy.92, f32[256,2,256]{0,2,1:T(8,128)} %copy.101, f32[256,2,256]{0,2,1:T(8,128)} %copy.96, f32[256,4,240]{0,2,1:T(8,128)} %get-tuple-element.188, f32[256,4,16]{0,2,1:T(8,128)S(1)} %get-tuple-element.190, f32[256,4,224]{0,2,1:T(8,128)} %get-tuple-element.184, ...), kind=kLoop, calls=%fused_computation.128 | loop fusion | flops 14942208 | bytes 15733504 | tf_op jit(solution)/shard_map/add | solution.py:98
  40.9 1.4 fusion.303
  42.3 1.5 fusion.305
  43.8 1.5 fusion.300
  46.7 1.5 fusion.301
  50.2 1.7 collective-permute-start.3
  52.8 1.5 fusion.297
  54.3 11.0 %collective-permute-done.3 = f32[256,2,256]{2,0,1:T(8,128)} collective-permute-done((f32[256,2,256]{2,0,1:T(8,128)}, f32[256,2,256]{2,0,1:T(8,128)}, u32[]{:S(2)}, u32[]{:S(2)}) %collective-permute-start.3) | collective-permute-done | bytes 524320 | tf_op jit(solution)/shard_map/ppermute | solution.py:26
  65.3 2.0 copy.130
  67.4 7.4 %collective-permute-done.2 = f32[256,2,256]{2,0,1:T(8,128)S(1)} collective-permute-done((f32[256,2,256]{2,0,1:T(8,128)S(1)}, f32[256,2,256]{2,0,1:T(8,128)S(1)}, u32[]{:S(2)}, u32[]{:S(2)}) %collective-permute-start.2) | collective-permute-done | bytes 524320 | tf_op jit(solution)/shard_map/ppermute | solution.py:25
  75.7 7.5 %fusion.87 = f32[256,4,256]{0,2,1:T(8,128)S(1)} fusion(f32[256,4,256]{0,2,1:T(8,128)S(1)} %fusion.104, f32[256,2,256]{0,2,1:T(8,128)} %copy.130, f32[256,2,256]{0,2,1:T(8,128)} %copy.128, f32[256,4,240]{0,2,1:T(8,128)} %get-tuple-element.162, f32[256,4,16]{0,2,1:T(8,128)S(1)} %get-tuple-element.164, f32[256,4,224]{0,2,1:T(8,128)} %get-tuple-element.158, ...), kind=kLoop, calls=%fused_computation.111 | loop fusion | flops 15728640 | bytes 16782080 | tf_op jit(solution)/shard_map/add | solution.py:99
  85.3 1.4 fusion.290
  86.7 1.5 fusion.292
  88.2 1.5 fusion.287
  89.7 1.4 fusion.283
  91.1 1.5 fusion.288
  94.6 1.5 collective-permute-start.5
  97.2 1.5 fusion.284
  98.7 11.0 %collective-permute-done.5 = f32[256,2,256]{2,0,1:T(8,128)} collective-permute-done((f32[256,2,256]{2,0,1:T(8,128)}, f32[256,2,256]{2,0,1:T(8,128)}, u32[]{:S(2)}, u32[]{:S(2)}) %collective-permute-start.5) | collective-permute-done | bytes 524320 | tf_op jit(solution)/shard_map/ppermute | solution.py:26
  109.7 2.0 copy.134
  111.8 6.5 %collective-permute-done.4 = f32[256,2,256]{2,0,1:T(8,128)S(1)} collective-permute-done((f32[256,2,256]{2,0,1:T(8,128)S(1)}, f32[256,2,256]{2,0,1:T(8,128)S(1)}, u32[]{:S(2)}, u32[]{:S(2)}) %collective-permute-start.4) | collective-permute-done | bytes 524320 | tf_op jit(solution)/shard_map/ppermute | solution.py:25
  119.3 7.5 %fusion.68 = f32[256,4,256]{0,2,1:T(8,128)S(1)} fusion(f32[256,4,256]{0,2,1:T(8,128)S(1)} %fusion.87, f32[256,2,256]{0,2,1:T(8,128)} %copy.134, f32[256,2,256]{0,2,1:T(8,128)} %copy.132, f32[256,4,240]{0,2,1:T(8,128)} %get-tuple-element.136, f32[256,4,16]{0,2,1:T(8,128)S(1)} %get-tuple-element.138, f32[256,4,224]{0,2,1:T(8,128)} %get-tuple-element.132, ...), kind=kLoop, calls=%fused_computation.92 | loop fusion | flops 15728640 | bytes 16782080 | tf_op jit(solution)/shard_map/add | solution.py:100
  127.8 58.6 %psum.14 = f32[5,1024]{1,0:T(8,128)S(1)} all-reduce(f32[5,1024]{1,0:T(8,128)S(1)} %fusion.208), channel_id=1, replica_groups=mesh['vel'=16,'gx'=2] {'vel'}, use_global_device_ids=true, to_apply=%region_0.1 | all-reduce | flops 5120 | bytes 40960 | tf_op jit(solution)/shard_map/psum | solution.py:138
  192.0 1.4 fusion.277
  193.4 1.5 fusion.279
  195.0 1.5 fusion.274
  196.4 1.4 fusion.270
  197.9 1.5 fusion.275
  201.4 1.5 collective-permute-start.7
  204.0 1.5 fusion.271
  205.4 11.0 %collective-permute-done.7 = f32[256,2,256]{2,0,1:T(8,128)} collective-permute-done((f32[256,2,256]{2,0,1:T(8,128)}, f32[256,2,256]{2,0,1:T(8,128)}, u32[]{:S(2)}, u32[]{:S(2)}) %collective-permute-start.7) | collective-permute-done | bytes 524320 | tf_op jit(solution)/shard_map/ppermute | solution.py:26
  216.5 2.0 copy.138
  218.5 3.6 collective-permute-done.6
  223.1 7.3 %fusion.49 = f32[256,4,256]{0,2,1:T(8,128)S(1)} fusion(f32[256,4,256]{0,2,1:T(8,128)S(1)} %add_divide_fusion.1, f32[256,2,256]{0,2,1:T(8,128)} %copy.138, f32[256,2,256]{0,2,1:T(8,128)} %copy.136, f32[256,4,240]{0,2,1:T(8,128)} %get-tuple-element.110, f32[256,4,16]{0,2,1:T(8,128)S(1)} %get-tuple-element.112, f32[256,4,224]{0,2,1:T(8,128)} %get-tuple-element.106, ...), kind=kLoop, calls=%fused_computation.73 | loop fusion | flops 14942208 | bytes 15733504 | tf_op jit(solution)/shard_map/add | solution.py:98
  234.0 1.5 fusion.266
  235.5 1.5 fusion.261
  237.0 1.4 fusion.257
  238.4 1.5 fusion.262
  241.9 1.5 collective-permute-start.9
  244.5 1.5 fusion.258
  246.0 10.3 %collective-permute-done.9 = f32[256,2,256]{2,0,1:T(8,128)} collective-permute-done((f32[256,2,256]{2,0,1:T(8,128)}, f32[256,2,256]{2,0,1:T(8,128)}, u32[]{:S(2)}, u32[]{:S(2)}) %collective-permute-start.9) | collective-permute-done | bytes 524320 | tf_op jit(solution)/shard_map/ppermute | solution.py:26
  256.3 2.0 copy.142
  258.3 3.5 collective-permute-done.8
  262.8 8.2 %fusion.32 = f32[256,4,256]{0,2,1:T(8,128)S(1)} fusion(f32[256,4,256]{0,2,1:T(8,128)S(1)} %fusion.49, f32[256,2,256]{0,2,1:T(8,128)} %copy.142, f32[256,2,256]{0,2,1:T(8,128)} %copy.140, f32[256,4,240]{0,2,1:T(8,128)} %get-tuple-element.84, f32[256,4,16]{0,2,1:T(8,128)S(1)} %get-tuple-element.86, f32[256,4,224]{0,2,1:T(8,128)} %get-tuple-element.80, ...), kind=kLoop, calls=%fused_computation.56 | loop fusion | flops 19660800 | bytes 16814848 | tf_op jit(solution)/shard_map/add | solution.py:99
  274.5 1.5 fusion.253
  276.0 1.5 fusion.248
  278.9 1.5 fusion.249
  282.4 1.5 collective-permute-start.11
  285.0 1.5 fusion.245
  286.5 9.5 %collective-permute-done.11 = f32[256,2,256]{2,0,1:T(8,128)} collective-permute-done((f32[256,2,256]{2,0,1:T(8,128)}, f32[256,2,256]{2,0,1:T(8,128)}, u32[]{:S(2)}, u32[]{:S(2)}) %collective-permute-start.11) | collective-permute-done | bytes 524320 | tf_op jit(solution)/shard_map/ppermute | solution.py:26
  296.0 2.0 copy.146
  298.0 3.5 collective-permute-done.10
  302.5 8.4 %fusion.13 = f32[256,4,256]{0,2,1:T(8,128)S(1)} fusion(f32[256,4,256]{0,2,1:T(8,128)S(1)} %fusion.32, f32[256,2,256]{0,2,1:T(8,128)} %copy.146, f32[256,2,256]{0,2,1:T(8,128)} %copy.144, f32[256,4,240]{0,2,1:T(8,128)} %get-tuple-element.58, f32[256,4,16]{0,2,1:T(8,128)S(1)} %get-tuple-element.60, f32[256,4,224]{0,2,1:T(8,128)} %get-tuple-element.54, ...), kind=kLoop, calls=%fused_computation.37 | loop fusion | flops 19660800 | bytes 16814848 | tf_op jit(solution)/shard_map/add | solution.py:100
  311.9 69.8 %psum.15 = f32[5,1024]{1,0:T(8,128)S(1)} all-reduce(f32[5,1024]{1,0:T(8,128)S(1)} %fusion.206), channel_id=1, replica_groups=mesh['vel'=16,'gx'=2] {'vel'}, use_global_device_ids=true, to_apply=%region_4.5 | all-reduce | flops 5120 | bytes 40960 | tf_op jit(solution)/shard_map/psum | solution.py:138
  (158 shorter events, 56.3 us)
Async XLA Ops:
  2.1 9.2 %copy-start = (f32[256,4,256]{2,1,0:T(4,128)S(1)}, f32[256,4,256]{2,1,0:T(4,128)}, u32[]{:S(2)}) copy-start(f32[256,4,256]{2,1,0:T(4,128)} %param.1) | copy-start | bytes 3145732
  2.9 19.9 %collective-permute-start.1 = (f32[256,2,256]{2,0,1:T(8,128)}, f32[256,2,256]{2,0,1:T(8,128)}, u32[]{:S(2)}, u32[]{:S(2)}) collective-permute-start(f32[256,2,256]{2,0,1:T(8,128)} %copy.149), channel_id=1, source_target_pairs={{1,0},{0,1},{3,2},{2,3},{5,4},{4,5},{7,6},{6,7},{9,8},{8,9},{11,10... | collective-permute-start | bytes 1572872 | tf_op jit(solution)/shard_map/ppermute | solution.py:26
  6.7 22.6 %collective-permute-start = (f32[256,2,256]{2,0,1:T(8,128)}, f32[256,2,256]{2,0,1:T(8,128)}, u32[]{:S(2)}, u32[]{:S(2)}) collective-permute-start(f32[256,2,256]{2,0,1:T(8,128)} %copy.148), channel_id=1, source_target_pairs={{0,1},{1,0},{2,3},{3,2},{4,5},{5,4},{6,7},{7,6},{8,9},{9,8},{10,11... | collective-permute-start | bytes 1572872 | tf_op jit(solution)/shard_map/ppermute | solution.py:25
  19.5 1.1 copy-start.16
  19.5 1.1 copy-start.17
  19.5 1.1 copy-start.18
  19.5 1.1 copy-start.19
  49.2 2.7 copy-start.1
  50.2 15.1 %collective-permute-start.3 = (f32[256,2,256]{2,0,1:T(8,128)}, f32[256,2,256]{2,0,1:T(8,128)}, u32[]{:S(2)}, u32[]{:S(2)}) collective-permute-start(f32[256,2,256]{2,0,1:T(8,128)} %copy.129), channel_id=1, source_target_pairs={{1,0},{0,1},{3,2},{2,3},{5,4},{4,5},{7,6},{6,7},{9,8},{8,9},{11,10... | collective-permute-start | bytes 1572872 | tf_op jit(solution)/shard_map/ppermute | solution.py:26
  51.9 22.8 %collective-permute-start.2 = (f32[256,2,256]{2,0,1:T(8,128)S(1)}, f32[256,2,256]{2,0,1:T(8,128)S(1)}, u32[]{:S(2)}, u32[]{:S(2)}) collective-permute-start(f32[256,2,256]{2,0,1:T(8,128)S(1)} %copy-done.1), channel_id=1, source_target_pairs={{0,1},{1,0},{2,3},{3,2},{4,5},{5,4},{6,7},{7,6},{8,9},{9,8},{10,11... | collective-permute-start | bytes 1572872 | tf_op jit(solution)/shard_map/ppermute | solution.py:25
  93.6 2.5 copy-start.2
  94.6 15.1 %collective-permute-start.5 = (f32[256,2,256]{2,0,1:T(8,128)}, f32[256,2,256]{2,0,1:T(8,128)}, u32[]{:S(2)}, u32[]{:S(2)}) collective-permute-start(f32[256,2,256]{2,0,1:T(8,128)} %copy.133), channel_id=1, source_target_pairs={{1,0},{0,1},{3,2},{2,3},{5,4},{4,5},{7,6},{6,7},{9,8},{8,9},{11,10... | collective-permute-start | bytes 1572872 | tf_op jit(solution)/shard_map/ppermute | solution.py:26
  96.1 22.2 %collective-permute-start.4 = (f32[256,2,256]{2,0,1:T(8,128)S(1)}, f32[256,2,256]{2,0,1:T(8,128)S(1)}, u32[]{:S(2)}, u32[]{:S(2)}) collective-permute-start(f32[256,2,256]{2,0,1:T(8,128)S(1)} %copy-done.2), channel_id=1, source_target_pairs={{0,1},{1,0},{2,3},{3,2},{4,5},{5,4},{6,7},{7,6},{8,9},{9,8},{10,11... | collective-permute-start | bytes 1572872 | tf_op jit(solution)/shard_map/ppermute | solution.py:25
  126.8 60.8 %copy-start.20 = (f32[16]{0:T(128)S(1)}, f32[16]{0:T(128)}, u32[]{:S(2)}) copy-start(f32[16]{0:T(128)} %multiply_add_fusion.9) | copy-start | bytes 196
  126.8 61.8 %copy-start.6 = (f32[256]{0:T(256)S(1)}, f32[256]{0:T(256)}, u32[]{:S(2)}) copy-start(f32[256]{0:T(256)} %fusion.228) | copy-start | bytes 3076
  187.5 2.3 copy-start.8
  187.5 2.3 copy-start.9
  187.6 2.3 copy-start.10
  187.8 2.1 copy-start.11
  187.9 2.0 copy-start.12
  187.9 2.0 copy-start.13
  188.5 1.4 copy-start.14
  188.6 1.4 copy-start.15
  200.4 2.5 copy-start.3
  201.4 15.1 %collective-permute-start.7 = (f32[256,2,256]{2,0,1:T(8,128)}, f32[256,2,256]{2,0,1:T(8,128)}, u32[]{:S(2)}, u32[]{:S(2)}) collective-permute-start(f32[256,2,256]{2,0,1:T(8,128)} %copy.137), channel_id=1, source_target_pairs={{1,0},{0,1},{3,2},{2,3},{5,4},{4,5},{7,6},{6,7},{9,8},{8,9},{11,10... | collective-permute-start | bytes 1572872 | tf_op jit(solution)/shard_map/ppermute | solution.py:26
  202.9 19.2 %collective-permute-start.6 = (f32[256,2,256]{2,0,1:T(8,128)S(1)}, f32[256,2,256]{2,0,1:T(8,128)S(1)}, u32[]{:S(2)}, u32[]{:S(2)}) collective-permute-start(f32[256,2,256]{2,0,1:T(8,128)S(1)} %copy-done.3), channel_id=1, source_target_pairs={{0,1},{1,0},{2,3},{3,2},{4,5},{5,4},{6,7},{7,6},{8,9},{9,8},{10,11... | collective-permute-start | bytes 1572872 | tf_op jit(solution)/shard_map/ppermute | solution.py:25
  240.9 2.5 copy-start.4
  241.9 14.4 %collective-permute-start.9 = (f32[256,2,256]{2,0,1:T(8,128)}, f32[256,2,256]{2,0,1:T(8,128)}, u32[]{:S(2)}, u32[]{:S(2)}) collective-permute-start(f32[256,2,256]{2,0,1:T(8,128)} %copy.141), channel_id=1, source_target_pairs={{1,0},{0,1},{3,2},{2,3},{5,4},{4,5},{7,6},{6,7},{9,8},{8,9},{11,10... | collective-permute-start | bytes 1572872 | tf_op jit(solution)/shard_map/ppermute | solution.py:26
  243.4 18.4 %collective-permute-start.8 = (f32[256,2,256]{2,0,1:T(8,128)S(1)}, f32[256,2,256]{2,0,1:T(8,128)S(1)}, u32[]{:S(2)}, u32[]{:S(2)}) collective-permute-start(f32[256,2,256]{2,0,1:T(8,128)S(1)} %copy-done.4), channel_id=1, source_target_pairs={{0,1},{1,0},{2,3},{3,2},{4,5},{5,4},{6,7},{7,6},{8,9},{9,8},{10,11... | collective-permute-start | bytes 1572872 | tf_op jit(solution)/shard_map/ppermute | solution.py:25
  281.4 2.5 copy-start.5
  282.4 13.6 %collective-permute-start.11 = (f32[256,2,256]{2,0,1:T(8,128)}, f32[256,2,256]{2,0,1:T(8,128)}, u32[]{:S(2)}, u32[]{:S(2)}) collective-permute-start(f32[256,2,256]{2,0,1:T(8,128)} %copy.145), channel_id=1, source_target_pairs={{1,0},{0,1},{3,2},{2,3},{5,4},{4,5},{7,6},{6,7},{9,8},{8,9},{11,10... | collective-permute-start | bytes 1572872 | tf_op jit(solution)/shard_map/ppermute | solution.py:26
  283.9 17.6 %collective-permute-start.10 = (f32[256,2,256]{2,0,1:T(8,128)S(1)}, f32[256,2,256]{2,0,1:T(8,128)S(1)}, u32[]{:S(2)}, u32[]{:S(2)}) collective-permute-start(f32[256,2,256]{2,0,1:T(8,128)S(1)} %copy-done.5), channel_id=1, source_target_pairs={{0,1},{1,0},{2,3},{3,2},{4,5},{5,4},{6,7},{7,6},{8,9},{9,8},{10,11... | collective-permute-start | bytes 1572872 | tf_op jit(solution)/shard_map/ppermute | solution.py:25
  311.0 71.5 %copy-start.21 = (f32[16]{0:T(128)S(1)}, f32[16]{0:T(128)}, u32[]{:S(2)}) copy-start(f32[16]{0:T(128)} %multiply_add_fusion.9) | copy-start | bytes 196
  311.0 72.4 %copy-start.7 = (f32[256]{0:T(256)S(1)}, f32[256]{0:T(256)}, u32[]{:S(2)}) copy-start(f32[256]{0:T(256)} %fusion.228) | copy-start | bytes 3076
where the time goes:
time: 387 us; the launch traced here: 386 us
  blocking collectives  128 us (33%)
  local copies, waits for them, and re-layouts  104 us (27%)
  waiting for transfers between devices  81.9 us (21%)
  other arithmetic  56.3 us (15%)
  starting transfers between devices  13.1 us (3%)
    psum x2, blocking collectives, collide(): prims = primitive(lax.psum(local, 'vel'))  128 us
    ppermute x6, waiting for transfers between devices, extended(): after = lax.ppermute(leading, axis, down)  52.9 us
    ppermute x6, waiting for transfers between devices, extended(): before = lax.ppermute(last, axis, up)  29 us
    slice x24, local copies, waits for them, and re-layouts, along_z(): other = jnp.roll(field, offset + NZ, -1)  25.4 us
    slice x24, local copies, waits for them, and re-layouts, along_z(): main = jnp.roll(field, offset, -1)  24.6 us
    add x2, other arithmetic, advance(): field / 3.0  15.9 us
    add x2, other arithmetic, advance(): 0.75 * field  15.6 us
    add x2, other arithmetic, advance(): first = field + time_step * rate(field, comp_x, comp_y, comp_z)  14.7 us
  transfers between devices with their start and end apart: 12, of which 11 were waited for; matrix products, arithmetic and copies ran while one was open for 10% of the time, Pallas kernels for 0%

commit v1 on v0

v1 whole, which is shorter than its diff:
```python
import functools
import math

import jax
import jax.numpy as jnp
from jax import lax
from jax.experimental import pallas as pl
from jax.experimental.pallas import tpu as pltpu
from jax.sharding import PartitionSpec as P

NV1 = 16
NZ = 16
COLLISIONS = 2
MOMENTS = 5
BLOCK = 4
MESH = pl.DeviceIdType.MESH

speed_limit = 4.0
time_step = 0.05
knudsen = 0.0125
spacing = 2.0 * speed_limit / (NV1 - 1)
weight = spacing**3 / (2.0 * math.pi) ** 1.5


def loop(count, body):
    def wrapped(i, carry):
        body(i)
        return carry

    lax.fori_loop(0, count, wrapped, 0)


def component(index):
    return -speed_limit + spacing * index.astype(jnp.float32)


def streamed(field, cx0, cy, cz):
    shape = field.shape
    nx, cells = shape[1], shape[2]
    ahead = (cx0 > 0, cy > 0, cz > 0)
    sx1 = jnp.where(ahead[0], 1, nx - 1)
    sx2 = jnp.where(ahead[0], 2, nx - 2)
    sy1 = jnp.where(ahead[1], NZ, cells - NZ)
    sy2 = jnp.where(ahead[1], 2 * NZ, cells - 2 * NZ)
    sz1 = jnp.where(ahead[2], 1, cells - 1)
    sz2 = jnp.where(ahead[2], 2, cells - 2)
    wz1 = jnp.where(ahead[2], cells + 1 - NZ, NZ - 1)
    wz2 = jnp.where(ahead[2], cells + 2 - NZ, NZ - 2)
    zpos = lax.broadcasted_iota(jnp.int32, shape, 2) % NZ
    depth = jnp.where(ahead[2], 0, NZ - 1) + jnp.where(ahead[2], 1, -1) * zpos
    keep1, keep2 = depth >= 1, depth >= 2
    half = 0.5 * time_step
    step = lax.broadcasted_iota(jnp.int32, shape, 0).astype(jnp.float32)
    kx = half * jnp.abs(cx0 + spacing * step)
    ky = half * jnp.abs(cy)
    kz = half * jnp.abs(cz)
    centre = 3.0 * (kx + (ky + kz))

    def change(g):
        x1, x2 = pltpu.roll(g, sx1, 1), pltpu.roll(g, sx2, 1)
        y1, y2 = pltpu.roll(g, sy1, 2), pltpu.roll(g, sy2, 2)
        z1 = jnp.where(keep1, pltpu.roll(g, sz1, 2), pltpu.roll(g, wz1, 2))
        z2 = jnp.where(keep2, pltpu.roll(g, sz2, 2), pltpu.roll(g, wz2, 2))
        gain = kx * (4.0 * x1 - x2) + ky * (4.0 * y1 - y2) + kz * (4.0 * z1 - z2)
        return gain - centre * g

    first = field + change(field)
    second = 0.75 * field + 0.25 * (first + change(first))
    return field * (1.0 / 3.0) + (2.0 / 3.0) * (second + change(second))


def fill_tables(moments, table, factor):
    rho = moments[0]
    ux, uy, uz = moments[1] / rho, moments[2] / rho, moments[3] / rho
    temp = (moments[4] / rho - (ux * ux + uy * uy + uz * uz)) / 3.0
    inverse = -0.5 / temp
    mass = None
    for d, u in enumerate((ux, uy, uz)):
        total = None
        for i in range(NV1):
            offset = (-speed_limit + spacing * i) - u
            value = jnp.exp(offset * offset * inverse)
            table[d, i] = value
            total = value if total is None else total + value
        mass = total if mass is None else mass * total
    nu = time_step * rho * jnp.sqrt(temp) / knudsen
    keep = 1.0 / (1.0 + nu)
    factor[0] = keep
    factor[1] = keep * nu * (rho / (weight * mass))


def kernel(
    nv, ng, src, out, slab, field, back, part, inbox, total, table, factor, table2, factor2,
    own_sem, in_send, in_recv, out_send, out_recv, rs_send, rs_recv, ag_send, ag_recv,
):
    count, xs, cells = src.shape
    n = count // ng
    nx = ng * xs
    nc = in_send.shape[1]
    size = n // nc
    ranks = nv * ng
    v, g = lax.axis_index("vel"), lax.axis_index("gx")
    me = v * ng + g

    barrier = pltpu.get_barrier_semaphore()

    def greet(i):
        other = lax.rem(me + i + 1, ranks)
        pl.semaphore_signal(barrier, 1, device_id=(other // ng, lax.rem(other, ng)), device_id_type=MESH)

    loop(ranks - 1, greet)
    own = pltpu.make_async_copy(src.at[pl.ds(g * n, n)], slab.at[g], own_sem)
    own.start()
    pl.semaphore_wait(barrier, ranks - 1)

    def incoming(d, c):
        to = lax.rem(g + d, ng)
        return pltpu.make_async_remote_copy(
            src_ref=src.at[pl.ds(to * n + c * size, size)],
            dst_ref=slab.at[g, pl.ds(c * size, size)],
            send_sem=in_send.at[d - 1, c],
            recv_sem=in_recv.at[d - 1, c],
            device_id=(v, to),
            device_id_type=MESH,
        )

    def outgoing(d, c):
        to = lax.rem(g + d, ng)
        return pltpu.make_async_remote_copy(
            src_ref=slab.at[to, pl.ds(c * size, size)],
            dst_ref=back.at[g, pl.ds(c * size, size)],
            send_sem=out_send.at[d - 1, c],
            recv_sem=out_recv.at[d - 1, c],
            device_id=(v, to),
            device_id_type=MESH,
        )

    def each(make, act, first=0, last=nc):
        def over(c):
            for d in range(1, ng):
                act(make(d, c + first))

        loop(last - first, over)

    each(incoming, lambda copy: copy.start())
    own.wait()

    def parts_of(k):
        ix = lax.rem(k, NV1)
        iz = lax.rem(k // NV1, NV1)
        iy = k // (NV1 * NV1)
        return ix, iy, iz

    def velocity_block(j, load, store, sums):
        ix, iy, iz = parts_of(v * count + g * n + j)
        cx0, cy, cz = component(ix), component(iy), component(iz)
        read = streamed(load(j, ix, iy, iz), cx0, cy, cz)
        store(j, read)
        s0 = s1 = s2 = None
        for b in range(BLOCK):
            cx = cx0 + spacing * b
            one = read[b]
            m1 = cx * one
            m2 = cx * m1
            s0 = one if s0 is None else s0 + one
            s1 = m1 if s1 is None else s1 + m1
            s2 = m2 if s2 is None else s2 + m2
        return (
            sums[0] + s0,
            sums[1] + s1,
            sums[2] + cy * s0,
            sums[3] + cz * s0,
            sums[4] + (s2 + (cy * cy + cz * cz) * s0),
        )

    def chunk(c, load, store, sums):
        def body(i, carry):
            return velocity_block(c * size + i * BLOCK, load, store, carry)

        return lax.fori_loop(0, size // BLOCK, body, sums)

    zero = tuple(jnp.zeros((nx, cells), jnp.float32) for _ in range(MOMENTS))
    owner = [(i * nv) // MOMENTS for i in range(MOMENTS)]
    is_owner = functools.reduce(jnp.logical_or, [v == o for o in owner])

    def write_part(which, sums):
        for i in range(MOMENTS):
            for s in range(ng):
                part[which, i, s] = weight * sums[i][s * xs : (s + 1) * xs]

    def scatter(which):
        for i, o in enumerate(owner):
            def over(s, i=i, o=o):
                @pl.when(jnp.logical_not(jnp.logical_and(v == o, g == s)))
                def _():
                    slot = lax.rem(me - (o * ng + s) - 1 + ranks, ranks)
                    pltpu.make_async_remote_copy(
                        src_ref=part.at[which, i, s],
                        dst_ref=inbox.at[which, slot],
                        send_sem=rs_send.at[which],
                        recv_sem=rs_recv.at[which],
                        device_id=(o, s),
                        device_id_type=MESH,
                    ).start()

            loop(ng, over)

    def local(ref, sem):
        return pltpu.make_async_copy(ref, ref, sem)

    def gather(which, everyone):
        peers = ranks if everyone else nv
        for i, o in enumerate(owner):
            @pl.when(v == o)
            def _(i=i):
                local(inbox.at[which], rs_recv.at[which]).wait()

                def add(k, acc):
                    return acc + inbox[which, k]

                acc = lax.fori_loop(0, ranks - 1, add, part[which, i, g])
                total[which, i * ng + g] = acc

                def send(k):
                    if everyone:
                        other = lax.rem(me + k + 1, ranks)
                        target = (other // ng, lax.rem(other, ng))
                    else:
                        target = (lax.rem(v + k + 1, nv), g)
                    pltpu.make_async_remote_copy(
                        src_ref=total.at[which, i * ng + g],
                        dst_ref=total.at[which, i * ng + g],
                        send_sem=ag_send.at[which],
                        recv_sem=ag_recv.at[which],
                        device_id=target,
                        device_id_type=MESH,
                    ).start()

                loop(peers - 1, send)

        items = MOMENTS * ng if everyone else MOMENTS

        @pl.when(is_owner)
        def _():
            local(total.at[which, pl.ds(0, items - 1)], ag_recv.at[which]).wait()

        @pl.when(jnp.logical_not(is_owner))
        def _():
            local(total.at[which, pl.ds(0, items)], ag_recv.at[which]).wait()

    def drain(which, everyone):
        peers = ranks if everyone else nv

        items = MOMENTS * ng

        @pl.when(is_owner)
        def _():
            local(total.at[which, pl.ds(0, items - 1)], rs_send.at[which]).wait()
            local(inbox.at[which, pl.ds(0, peers - 1)], ag_send.at[which]).wait()

        @pl.when(jnp.logical_not(is_owner))
        def _():
            local(total.at[which], rs_send.at[which]).wait()

    def load_first(j, ix, iy, iz):
        return jnp.concatenate([slab[s, pl.ds(j, BLOCK)] for s in range(ng)], axis=1)

    def store_first(j, read):
        field[pl.ds(j, BLOCK)] = read

    def first_chunk(c, sums):
        for d in range(1, ng):
            incoming(d, c).wait_recv()
        return chunk(c, load_first, store_first, sums)

    sums = lax.fori_loop(0, nc, first_chunk, zero)
    write_part(0, sums)
    scatter(0)
    each(incoming, lambda copy: copy.wait_send())
    gather(0, True)
    fill_tables(
        [jnp.concatenate([total[0, i * ng + s] for s in range(ng)], axis=0) for i in range(MOMENTS)],
        table,
        factor,
    )

    def load_second(j, ix, iy, iz):
        rest = factor[1] * table[1, iy] * table[2, iz]
        return factor[0] * field[pl.ds(j, BLOCK)] + rest * table[0, pl.ds(ix, BLOCK)]

    def store_second(j, read):
        for s in range(ng):
            slab[s, pl.ds(j, BLOCK)] = read[:, s * xs : (s + 1) * xs]

    early = nc // 2

    def second_chunk(c, sums):
        return chunk(c, load_second, store_second, sums)

    def second_sent(c, sums):
        sums = second_chunk(c, sums)
        for d in range(1, ng):
            outgoing(d, c).start()
        return sums

    sums = lax.fori_loop(0, early, second_sent, zero)
    sums = lax.fori_loop(early, nc, second_chunk, sums)
    write_part(1, sums)
    scatter(1)
    each(outgoing, lambda copy: copy.start(), early, nc)
    drain(0, True)
    gather(1, False)
    fill_tables([total[1, i * ng + g] for i in range(MOMENTS)], table2, factor2)

    def relax(source, s, c):
        def body(i):
            j = c * size + i * BLOCK
            ix, iy, iz = parts_of(v * count + s * n + j)
            rest = factor2[1] * table2[1, iy] * table2[2, iz]
            out[pl.ds(s * n + j, BLOCK)] = (
                factor2[0] * source[s, pl.ds(j, BLOCK)] + rest * table2[0, pl.ds(ix, BLOCK)]
            )

        loop(size // BLOCK, body)

    loop(nc, lambda c: relax(slab, g, c))

    def last(c):
        for d in range(1, ng):
            outgoing(d, c).wait_recv()
            relax(back, lax.rem(g - d + ng, ng), c)

    loop(nc, last)
    each(outgoing, lambda copy: copy.wait_send())
    drain(1, False)


def on_device(distribution):
    nv, ng = lax.axis_size("vel"), lax.axis_size("gx")
    count, xs, cells = distribution.shape
    n = count // ng
    nx = xs * ng
    size = max(BLOCK, n // 8)
    nc = n // size
    f32 = jnp.float32
    dma = pltpu.SemaphoreType.DMA
    return pl.pallas_call(
        functools.partial(kernel, nv, ng),
        out_shape=jax.ShapeDtypeStruct(distribution.shape, f32),
        in_specs=[pl.BlockSpec(memory_space=pl.ANY)],
        out_specs=pl.BlockSpec(memory_space=pltpu.VMEM),
        scratch_shapes=[
            pltpu.VMEM((ng, n, xs, cells), f32),
            pltpu.VMEM((n, nx, cells), f32),
            pltpu.VMEM((ng, n, xs, cells), f32),
            pltpu.VMEM((COLLISIONS, MOMENTS, ng, xs, cells), f32),
            pltpu.VMEM((COLLISIONS, nv * ng - 1, xs, cells), f32),
            pltpu.VMEM((COLLISIONS, MOMENTS * ng, xs, cells), f32),
            pltpu.VMEM((3, NV1, nx, cells), f32),
            pltpu.VMEM((2, nx, cells), f32),
            pltpu.VMEM((3, NV1, xs, cells), f32),
            pltpu.VMEM((2, xs, cells), f32),
            dma(()),
            dma((max(ng - 1, 1), nc)),
            dma((max(ng - 1, 1), nc)),
            dma((max(ng - 1, 1), nc)),
            dma((max(ng - 1, 1), nc)),
            dma((COLLISIONS,)),
            dma((COLLISIONS,)),
            dma((COLLISIONS,)),
            dma((COLLISIONS,)),
        ],
        compiler_params=pltpu.CompilerParams(collective_id=0, has_side_effects=True),
    )(distribution)


def solution(mesh):
    return jax.shard_map(
        on_device,
        mesh=mesh,
        in_specs=(P("vel", "gx", None),),
        out_specs=P("vel", "gx", None),
        check_vma=False,
    )
```

time: 387 us -> 58.1 us (0.15)
  blocking collectives: 128 us -> 0 us
  local copies, waits for them, and re-layouts: 104 us -> 2.37 us
  waiting for transfers between devices: 81.9 us -> 0 us
  other arithmetic: 56.3 us -> 0 us
  Pallas kernels: 0 us -> 55.5 us
  starting transfers between devices: 13.1 us -> 0 us
    psum x2 -> x0, blocking collectives: 128 us -> none  [collide(): prims = primitive(lax.psum(local, 'vel'))]
    ppermute x12 -> x0, waiting for transfers between devices: 81.9 us -> none  [the longest x6 52.9 us: extended(): after = lax.ppermute(leading, axis, down)]
    slice x88 -> x0, local copies, waits for them, and re-layouts: 80.3 us -> none  [the longest x24 25.4 us: along_z(): other = jnp.roll(field, offset + NZ, -1)]
    pallas_call x0 -> x1, Pallas kernels: none -> 55.5 us  [on_device(): pl.pallas_call(functools.partial(kernel, nv, ng), out_shape=jax.ShapeDtyp...]
    add x11 -> x0, other arithmetic: 48.5 us -> none  [the longest x2 15.9 us: advance(): field / 3.0]
    ppermute x12 -> x0, local copies, waits for them, and re-layouts: 19.3 us -> none  [the longest x6 12.2 us: extended(): after = lax.ppermute(leading, axis, down)]
    ppermute x12 -> x0, starting transfers between devices: 13.1 us -> none  [the longest x6 10.8 us: extended(): after = lax.ppermute(leading, axis, down)]
    div x6 -> x0, other arithmetic: 5.14 us -> none  [the longest x2 2.52 us: collide(): (flat + rates * (dense * scale)) / (1.0 + rates)]
  transfers between devices with their start and end apart: 12 -> 0, of which waited for: 11 -> 0; matrix products, arithmetic and copies ran while one was open for 10% -> 0% of each run, Pallas kernels for 0% -> 0%
where the time goes in v1:
time: 58.1 us; the launch traced here: 57.9 us
  Pallas kernels  55.5 us (96%)
  local copies, waits for them, and re-layouts  2.37 us (4%)
    pallas_call x1, Pallas kernels, on_device(): pl.pallas_call(functools.partial(kernel, nv, ng), out_shape=jax.ShapeDtyp...  55.5 us
    unnamed x1, local copies, waits for them, and re-layouts  2.37 us

profile of v1, /device:TPU:0, one launch (start us, length us, event | category | flops | bytes accessed | tf_op | source)
XLA Modules:
  0.0 57.9 jit_solution(2313496990576554023)
XLA Ops:
  0.0 55.5 %shard_map.17 = f32[256,4,256]{2,1,0:T(4,128)} custom-call(f32[256,4,256]{2,1,0:T(4,128)} %src.1), custom_call_target="tpu_custom_call" | custom-call | tf_op jit(solution)/shard_map/pallas_call | solution.py:347
  55.5 2.4 %copy.3 = f32[256,4,256]{2,1,0:T(4,128)} copy(f32[256,4,256]{2,1,0:T(4,128)} %shard_map.17) | data formatting | bytes 2097152

commit v2 on v1

--- a/solution.py
+++ b/solution.py
@@ -13,6 +13,7 @@
 COLLISIONS = 2
 MOMENTS = 5
 BLOCK = 4
+LANES = 128
 MESH = pl.DeviceIdType.MESH
 
 speed_limit = 4.0
@@ -34,39 +35,59 @@
     return -speed_limit + spacing * index.astype(jnp.float32)
 
 
-def streamed(field, cx0, cy, cz):
+def streamed(field, ix0, cy, cz):
     shape = field.shape
     nx, cells = shape[1], shape[2]
-    ahead = (cx0 > 0, cy > 0, cz > 0)
-    sx1 = jnp.where(ahead[0], 1, nx - 1)
-    sx2 = jnp.where(ahead[0], 2, nx - 2)
-    sy1 = jnp.where(ahead[1], NZ, cells - NZ)
-    sy2 = jnp.where(ahead[1], 2 * NZ, cells - 2 * NZ)
-    sz1 = jnp.where(ahead[2], 1, cells - 1)
-    sz2 = jnp.where(ahead[2], 2, cells - 2)
-    wz1 = jnp.where(ahead[2], cells + 1 - NZ, NZ - 1)
-    wz2 = jnp.where(ahead[2], cells + 2 - NZ, NZ - 2)
-    zpos = lax.broadcasted_iota(jnp.int32, shape, 2) % NZ
-    depth = jnp.where(ahead[2], 0, NZ - 1) + jnp.where(ahead[2], 1, -1) * zpos
-    keep1, keep2 = depth >= 1, depth >= 2
+    lanes = min(LANES, cells)
+    pieces = cells // lanes
+    fields = [field[:, :, h * lanes : (h + 1) * lanes] for h in range(pieces)]
+    shape = fields[0].shape
+    up_x = ix0 >= NV1 // 2
+    up_y, up_z = cy > 0, cz > 0
+    lane = lax.broadcasted_iota(jnp.int32, shape, 2)
+    zpos = lane % NZ
+    depth_z = jnp.where(up_z, 0, NZ - 1) + jnp.where(up_z, 1, -1) * zpos
+    depth_y = jnp.where(up_y, 0, lanes - 1) + jnp.where(up_y, 1, -1) * lane
     half = 0.5 * time_step
-    step = lax.broadcasted_iota(jnp.int32, shape, 0).astype(jnp.float32)
-    kx = half * jnp.abs(cx0 + spacing * step)
-    ky = half * jnp.abs(cy)
-    kz = half * jnp.abs(cz)
-    centre = 3.0 * (kx + (ky + kz))
-
-    def change(g):
-        x1, x2 = pltpu.roll(g, sx1, 1), pltpu.roll(g, sx2, 1)
-        y1, y2 = pltpu.roll(g, sy1, 2), pltpu.roll(g, sy2, 2)
-        z1 = jnp.where(keep1, pltpu.roll(g, sz1, 2), pltpu.roll(g, wz1, 2))
-        z2 = jnp.where(keep2, pltpu.roll(g, sz2, 2), pltpu.roll(g, wz2, 2))
-        gain = kx * (4.0 * x1 - x2) + ky * (4.0 * y1 - y2) + kz * (4.0 * z1 - z2)
-        return gain - centre * g
-
-    first = field + change(field)
-    second = 0.75 * field + 0.25 * (first + change(first))
-    return field * (1.0 / 3.0) + (2.0 / 3.0) * (second + change(second))
+    speeds = [abs(-speed_limit + spacing * (ix0 + b)) for b in range(shape[0])]
+    ay, az = jnp.abs(cy), jnp.abs(cz)
+    amount_y = [jnp.where(up_y, k * NZ, lanes - k * NZ) for k in (1, 2)]
+    amount_z = [jnp.where(up_z, k, lanes - k) for k in (1, 2)]
+    wrap_z = [jnp.where(up_z, lanes + k - NZ, NZ - k) for k in (1, 2)]
+    keep_y = [depth_y >= k * NZ for k in (1, 2)]
+    keep_z = [depth_z >= k for k in (1, 2)]
+
+    def advanced(gs, factor):
+        scale = factor * half
+        ky, kz = scale * ay, scale * az
+        kx = [scale * speed for speed in speeds]
+        centre = [3.0 * (k + (ky + kz)) for k in kx]
+        spread = lambda values: jnp.stack([jnp.full(shape[1:], k, jnp.float32) for k in values])
+        kx, centre = spread(kx), spread(centre)
+        fours = [4.0 * g for g in gs]
+        y1 = [pltpu.roll(g, amount_y[0], 2) for g in fours]
+        y2 = [pltpu.roll(g, amount_y[1], 2) for g in gs]
+
+        def across(turned, h, keep):
+            if pieces == 1:
+                return turned[h]
+            if pieces == 2:
+                return jnp.where(keep, turned[h], turned[1 - h])
+            other = jnp.where(up_y, turned[h - 1], turned[(h + 1) % pieces])
+            return jnp.where(keep, turned[h], other)
+
+        result = []
+        for h, (f, g, four) in enumerate(zip(fields, gs, fours)):
+            dx = pltpu.roll(four, 1 if up_x else nx - 1, 1) - pltpu.roll(g, 2 if up_x else nx - 2, 1)
+            dy = across(y1, h, keep_y[0]) - across(y2, h, keep_y[1])
+            z1 = jnp.where(keep_z[0], pltpu.roll(four, amount_z[0], 2), pltpu.roll(four, wrap_z[0], 2))
+            z2 = jnp.where(keep_z[1], pltpu.roll(g, amount_z[1], 2), pltpu.roll(g, wrap_z[1], 2))
+            result.append((f - centre * g) + kx * dx + ky * dy + kz * (z1 - z2))
+        return result
+
+    value = advanced(fields, 1.0 / 3.0)
+    value = advanced(value, 0.5)
+    return advanced(value, 1.0)
 
 
 def fill_tables(moments, table, factor):
@@ -151,20 +172,22 @@
         iy = k // (NV1 * NV1)
         return ix, iy, iz
 
-    def velocity_block(j, load, store, sums):
-        ix, iy, iz = parts_of(v * count + g * n + j)
-        cx0, cy, cz = component(ix), component(iy), component(iz)
-        read = streamed(load(j, ix, iy, iz), cx0, cy, cz)
-        store(j, read)
+    def velocity_row(j, load, store, sums):
+        _, iy, iz = parts_of(v * count + g * n + j)
+        cy, cz = component(iy), component(iz)
+        rest = load.prepare(iy, iz) if hasattr(load, "prepare") else None
         s0 = s1 = s2 = None
-        for b in range(BLOCK):
-            cx = cx0 + spacing * b
-            one = read[b]
-            m1 = cx * one
-            m2 = cx * m1
-            s0 = one if s0 is None else s0 + one
-            s1 = m1 if s1 is None else s1 + m1
-            s2 = m2 if s2 is None else s2 + m2
+        for ix in range(0, NV1, BLOCK):
+            read = jnp.concatenate(streamed(load(j + ix, ix, rest), ix, cy, cz), axis=2)
+            store(j + ix, read)
+            for b in range(BLOCK):
+                cx = -speed_limit + spacing * (ix + b)
+                one = read[b]
+                m1 = cx * one
+                m2 = cx * m1
+                s0 = one if s0 is None else s0 + one
+                s1 = m1 if s1 is None else s1 + m1
+                s2 = m2 if s2 is None else s2 + m2
         return (
             sums[0] + s0,
             sums[1] + s1,
@@ -175,9 +198,9 @@
 
     def chunk(c, load, store, sums):
         def body(i, carry):
-            return velocity_block(c * size + i * BLOCK, load, store, carry)
-
-        return lax.fori_loop(0, size // BLOCK, body, sums)
+            return velocity_row(c * size + i * NV1, load, store, carry)
+
+        return lax.fori_loop(0, size // NV1, body, sums)
 
     zero = tuple(jnp.zeros((nx, cells), jnp.float32) for _ in range(MOMENTS))
     owner = [(i * nv) // MOMENTS for i in range(MOMENTS)]
@@ -262,7 +285,7 @@
         def _():
             local(total.at[which], rs_send.at[which]).wait()
 
-    def load_first(j, ix, iy, iz):
+    def load_first(j, ix, rest):
         return jnp.concatenate([slab[s, pl.ds(j, BLOCK)] for s in range(ng)], axis=1)
 
     def store_first(j, read):
@@ -284,9 +307,10 @@
         factor,
     )
 
-    def load_second(j, ix, iy, iz):
-        rest = factor[1] * table[1, iy] * table[2, iz]
-        return factor[0] * field[pl.ds(j, BLOCK)] + rest * table[0, pl.ds(ix, BLOCK)]
+    def load_second(j, ix, rest):
+        return factor[0] * field[pl.ds(j, BLOCK)] + rest * table[0, ix : ix + BLOCK]
+
+    load_second.prepare = lambda iy, iz: factor[1] * table[1, iy] * table[2, iz]
 
     def store_second(j, read):
         for s in range(ng):
@@ -314,14 +338,15 @@
 
     def relax(source, s, c):
         def body(i):
-            j = c * size + i * BLOCK
-            ix, iy, iz = parts_of(v * count + s * n + j)
+            j = c * size + i * NV1
+            _, iy, iz = parts_of(v * count + s * n + j)
             rest = factor2[1] * table2[1, iy] * table2[2, iz]
-            out[pl.ds(s * n + j, BLOCK)] = (
-                factor2[0] * source[s, pl.ds(j, BLOCK)] + rest * table2[0, pl.ds(ix, BLOCK)]
-            )
-
-        loop(size // BLOCK, body)
+            for ix in range(0, NV1, BLOCK):
+                out[pl.ds(s * n + j + ix, BLOCK)] = (
+                    factor2[0] * source[s, pl.ds(j + ix, BLOCK)] + rest * table2[0, ix : ix + BLOCK]
+                )
+
+        loop(size // NV1, body)
 
     loop(nc, lambda c: relax(slab, g, c))
 
@@ -340,13 +365,13 @@
     count, xs, cells = distribution.shape
     n = count // ng
     nx = xs * ng
-    size = max(BLOCK, n // 8)
+    size = max(NV1, n // 8)
     nc = n // size
     f32 = jnp.float32
     dma = pltpu.SemaphoreType.DMA
     return pl.pallas_call(
         functools.partial(kernel, nv, ng),
-        out_shape=jax.ShapeDtypeStruct(distribution.shape, f32),
+        out_shape=pltpu.VMEM(distribution.shape, f32),
         in_specs=[pl.BlockSpec(memory_space=pl.ANY)],
         out_specs=pl.BlockSpec(memory_space=pltpu.VMEM),
         scratch_shapes=[

time: 58.1 us -> 51 us (0.88)
  Pallas kernels: 55.5 us -> 49.8 us
  local copies, waits for them, and re-layouts: 2.37 us -> 0.97 us
    pallas_call x1, Pallas kernels: 55.5 us -> 49.8 us  [on_device(): pl.pallas_call(functools.partial(kernel, nv, ng), out_shape=pltpu.VMEM(di...]
    unnamed x1, local copies, waits for them, and re-layouts: 2.37 us -> 0.97 us
where the time goes in v2:
time: 51 us; the launch traced here: 50.8 us
  Pallas kernels  49.8 us (98%)
  local copies, waits for them, and re-layouts  0.97 us (2%)
    pallas_call x1, Pallas kernels, on_device(): pl.pallas_call(functools.partial(kernel, nv, ng), out_shape=pltpu.VMEM(di...  49.8 us

profile of v2, /device:TPU:0, one launch (start us, length us, event | category | flops | bytes accessed | tf_op | source)
XLA Modules:
  0.0 50.8 jit_solution(9523041879840647816)
XLA Ops:
  0.0 49.8 %shard_map.17 = f32[256,4,256]{2,1,0:T(4,128)S(1)} custom-call(f32[256,4,256]{2,1,0:T(4,128)} %src.1), custom_call_target="tpu_custom_call" | custom-call | tf_op jit(solution)/shard_map/pallas_call | solution.py:372
  49.9 1.0 %copy.3 = f32[256,4,256]{2,1,0:T(4,128)} copy(f32[256,4,256]{2,1,0:T(4,128)S(1)} %shard_map.17) | data formatting | bytes 2097152

commit v3 on v2

--- a/solution.py
+++ b/solution.py
@@ -12,8 +12,7 @@
 NZ = 16
 COLLISIONS = 2
 MOMENTS = 5
-BLOCK = 4
-LANES = 128
+BLOCK = 16
 MESH = pl.DeviceIdType.MESH
 
 speed_limit = 4.0
@@ -31,61 +30,73 @@
     lax.fori_loop(0, count, wrapped, 0)
 
 
+def far_first(size, body):
+    if size > 64:
+        loop(size - 1, lambda k: body(k + 1))
+        return
+    for gap in sorted(range(1, size), key=lambda gap: -min(gap, size - gap)):
+        body(gap)
+
+
 def component(index):
     return -speed_limit + spacing * index.astype(jnp.float32)
 
 
-def streamed(field, ix0, cy, cz):
-    shape = field.shape
-    nx, cells = shape[1], shape[2]
-    lanes = min(LANES, cells)
-    pieces = cells // lanes
-    fields = [field[:, :, h * lanes : (h + 1) * lanes] for h in range(pieces)]
-    shape = fields[0].shape
-    up_x = ix0 >= NV1 // 2
-    up_y, up_z = cy > 0, cz > 0
-    lane = lax.broadcasted_iota(jnp.int32, shape, 2)
-    zpos = lane % NZ
-    depth_z = jnp.where(up_z, 0, NZ - 1) + jnp.where(up_z, 1, -1) * zpos
-    depth_y = jnp.where(up_y, 0, lanes - 1) + jnp.where(up_y, 1, -1) * lane
+def fill_shifts(shifts):
+    cells = shifts.shape[1]
+    source = lax.broadcasted_iota(jnp.int32, (cells, cells), 0)
+    target = lax.broadcasted_iota(jnp.int32, (cells, cells), 1)
+    same = source // NZ == target // NZ
+    for way in (0, 1):
+        gap = target - source if way else source - target
+        along_y = lax.rem(gap + cells, cells)
+        along_z = lax.rem(gap + cells, NZ)
+        for d, (one, two) in enumerate(
+            (
+                (along_y == NZ, along_y == 2 * NZ),
+                (same & (along_z == 1), same & (along_z == 2)),
+            )
+        ):
+            value = jnp.where(one, 4.0, jnp.where(two, -1.0, 0.0))
+            shifts[2 * d + way] = value.astype(jnp.bfloat16)
+
+
+def streamed(field, ix0, cy, cz, shifts):
+    rows, nx, cells = field.shape
+    shape = (rows, nx, cells)
     half = 0.5 * time_step
-    speeds = [abs(-speed_limit + spacing * (ix0 + b)) for b in range(shape[0])]
+    speeds = [abs(-speed_limit + spacing * (ix0 + b)) for b in range(rows)]
+    signs = [ix0 + b >= NV1 // 2 for b in range(rows)]
+    low = signs.count(False)
     ay, az = jnp.abs(cy), jnp.abs(cz)
-    amount_y = [jnp.where(up_y, k * NZ, lanes - k * NZ) for k in (1, 2)]
-    amount_z = [jnp.where(up_z, k, lanes - k) for k in (1, 2)]
-    wrap_z = [jnp.where(up_z, lanes + k - NZ, NZ - k) for k in (1, 2)]
-    keep_y = [depth_y >= k * NZ for k in (1, 2)]
-    keep_z = [depth_z >= k for k in (1, 2)]
-
-    def advanced(gs, factor):
+    along_y = shifts[(cy > 0).astype(jnp.int32)]
+    along_z = shifts[2 + (cz > 0).astype(jnp.int32)]
+
+    def moved(g, k):
+        below = [pltpu.roll(g[:low], nx - k, 1)] if low else []
+        above = [pltpu.roll(g[low:], k, 1)] if low < rows else []
+        return jnp.concatenate(below + above, axis=0)
+
+    def advanced(g, factor):
         scale = factor * half
         ky, kz = scale * ay, scale * az
         kx = [scale * speed for speed in speeds]
         centre = [3.0 * (k + (ky + kz)) for k in kx]
         spread = lambda values: jnp.stack([jnp.full(shape[1:], k, jnp.float32) for k in values])
         kx, centre = spread(kx), spread(centre)
-        fours = [4.0 * g for g in gs]
-        y1 = [pltpu.roll(g, amount_y[0], 2) for g in fours]
-        y2 = [pltpu.roll(g, amount_y[1], 2) for g in gs]
-
-        def across(turned, h, keep):
-            if pieces == 1:
-                return turned[h]
-            if pieces == 2:
-                return jnp.where(keep, turned[h], turned[1 - h])
-            other = jnp.where(up_y, turned[h - 1], turned[(h + 1) % pieces])
-            return jnp.where(keep, turned[h], other)
-
-        result = []
-        for h, (f, g, four) in enumerate(zip(fields, gs, fours)):
-            dx = pltpu.roll(four, 1 if up_x else nx - 1, 1) - pltpu.roll(g, 2 if up_x else nx - 2, 1)
-            dy = across(y1, h, keep_y[0]) - across(y2, h, keep_y[1])
-            z1 = jnp.where(keep_z[0], pltpu.roll(four, amount_z[0], 2), pltpu.roll(four, wrap_z[0], 2))
-            z2 = jnp.where(keep_z[1], pltpu.roll(g, amount_z[1], 2), pltpu.roll(g, wrap_z[1], 2))
-            result.append((f - centre * g) + kx * dx + ky * dy + kz * (z1 - z2))
-        return result
-
-    value = advanced(fields, 1.0 / 3.0)
+        flat = g.reshape(rows * nx, cells)
+        top = flat.astype(jnp.bfloat16)
+        rest = (flat - top.astype(jnp.float32)).astype(jnp.bfloat16)
+        both = jnp.concatenate([top, rest], axis=0)
+
+        def apply(matrix):
+            d = jnp.dot(both, matrix, preferred_element_type=jnp.float32)
+            return (d[: rows * nx] + d[rows * nx :]).reshape(shape)
+
+        dx = 4.0 * moved(g, 1) - moved(g, 2)
+        return (field - centre * g) + kx * dx + ky * apply(along_y) + kz * apply(along_z)
+
+    value = advanced(field, 1.0 / 3.0)
     value = advanced(value, 0.5)
     return advanced(value, 1.0)
 
@@ -111,7 +122,7 @@
 
 
 def kernel(
-    nv, ng, src, out, slab, field, back, part, inbox, total, table, factor, table2, factor2,
+    nv, ng, src, out, slab, field, back, part, inbox, total, table, factor, table2, factor2, shifts,
     own_sem, in_send, in_recv, out_send, out_recv, rs_send, rs_recv, ag_send, ag_recv,
 ):
     count, xs, cells = src.shape
@@ -125,13 +136,14 @@
 
     barrier = pltpu.get_barrier_semaphore()
 
-    def greet(i):
-        other = lax.rem(me + i + 1, ranks)
+    def greet(gap):
+        other = lax.rem(me + gap, ranks)
         pl.semaphore_signal(barrier, 1, device_id=(other // ng, lax.rem(other, ng)), device_id_type=MESH)
 
-    loop(ranks - 1, greet)
+    far_first(ranks, greet)
     own = pltpu.make_async_copy(src.at[pl.ds(g * n, n)], slab.at[g], own_sem)
     own.start()
+    fill_shifts(shifts)
     pl.semaphore_wait(barrier, ranks - 1)
 
     def incoming(d, c):
@@ -178,7 +190,7 @@
         rest = load.prepare(iy, iz) if hasattr(load, "prepare") else None
         s0 = s1 = s2 = None
         for ix in range(0, NV1, BLOCK):
-            read = jnp.concatenate(streamed(load(j + ix, ix, rest), ix, cy, cz), axis=2)
+            read = streamed(load(j + ix, ix, rest), ix, cy, cz, shifts)
             store(j + ix, read)
             for b in range(BLOCK):
                 cx = -speed_limit + spacing * (ix + b)
@@ -233,33 +245,36 @@
 
     def gather(which, everyone):
         peers = ranks if everyone else nv
-        for i, o in enumerate(owner):
-            @pl.when(v == o)
-            def _(i=i):
-                local(inbox.at[which], rs_recv.at[which]).wait()
-
-                def add(k, acc):
-                    return acc + inbox[which, k]
-
-                acc = lax.fori_loop(0, ranks - 1, add, part[which, i, g])
-                total[which, i * ng + g] = acc
-
-                def send(k):
-                    if everyone:
-                        other = lax.rem(me + k + 1, ranks)
-                        target = (other // ng, lax.rem(other, ng))
-                    else:
-                        target = (lax.rem(v + k + 1, nv), g)
-                    pltpu.make_async_remote_copy(
-                        src_ref=total.at[which, i * ng + g],
-                        dst_ref=total.at[which, i * ng + g],
-                        send_sem=ag_send.at[which],
-                        recv_sem=ag_recv.at[which],
-                        device_id=target,
-                        device_id_type=MESH,
-                    ).start()
-
-                loop(peers - 1, send)
+
+        @pl.when(is_owner)
+        def _():
+            i = functools.reduce(jnp.add, [(v > o).astype(jnp.int32) for o in owner])
+            local(inbox.at[which], rs_recv.at[which]).wait()
+            lanes = [part[which, i, g]] + [jnp.zeros((xs, cells), jnp.float32)] * 3
+            if ranks <= 64:
+                for k in range(ranks - 1):
+                    lanes[k % 4] = lanes[k % 4] + inbox[which, k]
+                acc = (lanes[0] + lanes[1]) + (lanes[2] + lanes[3])
+            else:
+                acc = lax.fori_loop(0, ranks - 1, lambda k, acc: acc + inbox[which, k], lanes[0])
+            total[which, i * ng + g] = acc
+
+            def send(gap):
+                if everyone:
+                    other = lax.rem(me + gap, ranks)
+                    target = (other // ng, lax.rem(other, ng))
+                else:
+                    target = (lax.rem(v + gap, nv), g)
+                pltpu.make_async_remote_copy(
+                    src_ref=total.at[which, i * ng + g],
+                    dst_ref=total.at[which, i * ng + g],
+                    send_sem=ag_send.at[which],
+                    recv_sem=ag_recv.at[which],
+                    device_id=target,
+                    device_id_type=MESH,
+                ).start()
+
+            far_first(peers, send)
 
         items = MOMENTS * ng if everyone else MOMENTS
 
@@ -385,6 +400,7 @@
             pltpu.VMEM((2, nx, cells), f32),
             pltpu.VMEM((3, NV1, xs, cells), f32),
             pltpu.VMEM((2, xs, cells), f32),
+            pltpu.VMEM((4, cells, cells), jnp.bfloat16),
             dma(()),
             dma((max(ng - 1, 1), nc)),
             dma((max(ng - 1, 1), nc)),

time: 51 us -> 45.6 us (0.89)
  Pallas kernels: 49.8 us -> 44.5 us
    pallas_call x1, Pallas kernels: 49.8 us -> 44.5 us  [on_device(): pl.pallas_call(functools.partial(kernel, nv, ng), out_shape=pltpu.VMEM(di...]
where the time goes in v3:
time: 45.6 us; the launch traced here: 45.5 us
  Pallas kernels  44.5 us (98%)
  local copies, waits for them, and re-layouts  0.97 us (2%)
    pallas_call x1, Pallas kernels, on_device(): pl.pallas_call(functools.partial(kernel, nv, ng), out_shape=pltpu.VMEM(di...  44.5 us
    unnamed x1, local copies, waits for them, and re-layouts  0.97 us

profile of v3, /device:TPU:0, one launch (start us, length us, event | category | flops | bytes accessed | tf_op | source)
XLA Modules:
  0.0 45.5 jit_solution(14010791917131814066)
XLA Ops:
  0.0 44.5 %shard_map.17 = f32[256,4,256]{2,1,0:T(4,128)S(1)} custom-call(f32[256,4,256]{2,1,0:T(4,128)} %src.1), custom_call_target="tpu_custom_call" | custom-call | tf_op jit(solution)/shard_map/pallas_call | solution.py:387
  44.5 1.0 %copy.3 = f32[256,4,256]{2,1,0:T(4,128)} copy(f32[256,4,256]{2,1,0:T(4,128)S(1)} %shard_map.17) | data formatting | bytes 2097152

commit v4 on v3

--- a/solution.py
+++ b/solution.py
@@ -122,8 +122,8 @@
 
 
 def kernel(
-    nv, ng, src, out, slab, field, back, part, inbox, total, table, factor, table2, factor2, shifts,
-    own_sem, in_send, in_recv, out_send, out_recv, rs_send, rs_recv, ag_send, ag_recv,
+    nv, ng, src, out, slab, field, back, part, inbox0, total0, inbox1, total1, table, factor, table2, factor2, shifts,
+    known, own_sem, in_send, in_recv, out_send, out_recv, rs_send, rs_recv, ag_send, ag_recv,
 ):
     count, xs, cells = src.shape
     n = count // ng
@@ -136,15 +136,26 @@
 
     barrier = pltpu.get_barrier_semaphore()
 
-    def greet(gap):
-        other = lax.rem(me + gap, ranks)
-        pl.semaphore_signal(barrier, 1, device_id=(other // ng, lax.rem(other, ng)), device_id_type=MESH)
-
-    far_first(ranks, greet)
+    bits = ranks.bit_length() - 1
+    assert ranks == 1 << bits
+
+    def across(bit):
+        other = me + (1 << bit) * (1 - 2 * lax.rem(me // (1 << bit), 2))
+        return (other // ng, lax.rem(other, ng))
+
+    def rounds(first, last):
+        for bit in range(first, last):
+            pl.semaphore_signal(known.at[bit], 1, device_id=across(bit), device_id_type=MESH)
+            pl.semaphore_wait(known.at[bit], 1)
+
+    for bit in range(bits):
+        pl.semaphore_signal(barrier, 1, device_id=across(bit), device_id_type=MESH)
     own = pltpu.make_async_copy(src.at[pl.ds(g * n, n)], slab.at[g], own_sem)
     own.start()
     fill_shifts(shifts)
-    pl.semaphore_wait(barrier, ranks - 1)
+    pl.semaphore_wait(barrier, bits)
+    near = 0 if ng <= 2 else ng.bit_length() - 1
+    rounds(0, near)
 
     def incoming(d, c):
         to = lax.rem(g + d, ng)
@@ -176,6 +187,7 @@
         loop(last - first, over)
 
     each(incoming, lambda copy: copy.start())
+    rounds(near, bits)
     own.wait()
 
     def parts_of(k):
@@ -223,6 +235,11 @@
             for s in range(ng):
                 part[which, i, s] = weight * sums[i][s * xs : (s + 1) * xs]
 
+    inboxes, totals = (inbox0, inbox1), (total0, total1)
+
+    def piece(which, i, s):
+        return part.at[0, i] if which == 0 else part.at[1, i, s]
+
     def scatter(which):
         for i, o in enumerate(owner):
             def over(s, i=i, o=o):
@@ -230,8 +247,8 @@
                 def _():
                     slot = lax.rem(me - (o * ng + s) - 1 + ranks, ranks)
                     pltpu.make_async_remote_copy(
-                        src_ref=part.at[which, i, s],
-                        dst_ref=inbox.at[which, slot],
+                        src_ref=piece(which, i, s),
+                        dst_ref=inboxes[which].at[slot],
                         send_sem=rs_send.at[which],
                         recv_sem=rs_recv.at[which],
                         device_id=(o, s),
@@ -243,62 +260,51 @@
     def local(ref, sem):
         return pltpu.make_async_copy(ref, ref, sem)
 
-    def gather(which, everyone):
-        peers = ranks if everyone else nv
+    def gather(which):
+        inbox, total = inboxes[which], totals[which]
 
         @pl.when(is_owner)
         def _():
             i = functools.reduce(jnp.add, [(v > o).astype(jnp.int32) for o in owner])
-            local(inbox.at[which], rs_recv.at[which]).wait()
-            lanes = [part[which, i, g]] + [jnp.zeros((xs, cells), jnp.float32)] * 3
+            local(inbox, rs_recv.at[which]).wait()
+            lanes = [piece(which, i, g)[...]]
+            lanes += [jnp.zeros(lanes[0].shape, jnp.float32)] * 3
             if ranks <= 64:
                 for k in range(ranks - 1):
-                    lanes[k % 4] = lanes[k % 4] + inbox[which, k]
+                    lanes[k % 4] = lanes[k % 4] + inbox[k]
                 acc = (lanes[0] + lanes[1]) + (lanes[2] + lanes[3])
             else:
-                acc = lax.fori_loop(0, ranks - 1, lambda k, acc: acc + inbox[which, k], lanes[0])
-            total[which, i * ng + g] = acc
+                acc = lax.fori_loop(0, ranks - 1, lambda k, acc: acc + inbox[k], lanes[0])
+            total[i] = acc
 
             def send(gap):
-                if everyone:
-                    other = lax.rem(me + gap, ranks)
-                    target = (other // ng, lax.rem(other, ng))
-                else:
-                    target = (lax.rem(v + gap, nv), g)
                 pltpu.make_async_remote_copy(
-                    src_ref=total.at[which, i * ng + g],
-                    dst_ref=total.at[which, i * ng + g],
+                    src_ref=total.at[i],
+                    dst_ref=total.at[i],
                     send_sem=ag_send.at[which],
                     recv_sem=ag_recv.at[which],
-                    device_id=target,
+                    device_id=(lax.rem(v + gap, nv), g),
                     device_id_type=MESH,
                 ).start()
 
-            far_first(peers, send)
-
-        items = MOMENTS * ng if everyone else MOMENTS
+            far_first(nv, send)
+            local(total.at[pl.ds(0, MOMENTS - 1)], ag_recv.at[which]).wait()
+
+        @pl.when(jnp.logical_not(is_owner))
+        def _():
+            local(total, ag_recv.at[which]).wait()
+
+    def drain(which):
+        inbox = inboxes[which]
 
         @pl.when(is_owner)
         def _():
-            local(total.at[which, pl.ds(0, items - 1)], ag_recv.at[which]).wait()
+            local(inbox.at[pl.ds(0, MOMENTS * ng - 1)], rs_send.at[which]).wait()
+            local(inbox.at[pl.ds(0, nv - 1)], ag_send.at[which]).wait()
 
         @pl.when(jnp.logical_not(is_owner))
         def _():
-            local(total.at[which, pl.ds(0, items)], ag_recv.at[which]).wait()
-
-    def drain(which, everyone):
-        peers = ranks if everyone else nv
-
-        items = MOMENTS * ng
-
-        @pl.when(is_owner)
-        def _():
-            local(total.at[which, pl.ds(0, items - 1)], rs_send.at[which]).wait()
-            local(inbox.at[which, pl.ds(0, peers - 1)], ag_send.at[which]).wait()
-
-        @pl.when(jnp.logical_not(is_owner))
-        def _():
-            local(total.at[which], rs_send.at[which]).wait()
+            local(inbox.at[pl.ds(0, MOMENTS * ng)], rs_send.at[which]).wait()
 
     def load_first(j, ix, rest):
         return jnp.concatenate([slab[s, pl.ds(j, BLOCK)] for s in range(ng)], axis=1)
@@ -315,9 +321,9 @@
     write_part(0, sums)
     scatter(0)
     each(incoming, lambda copy: copy.wait_send())
-    gather(0, True)
+    gather(0)
     fill_tables(
-        [jnp.concatenate([total[0, i * ng + s] for s in range(ng)], axis=0) for i in range(MOMENTS)],
+        [jnp.concatenate([total0[i, s] for s in range(ng)], axis=0) for i in range(MOMENTS)],
         table,
         factor,
     )
@@ -347,9 +353,9 @@
     write_part(1, sums)
     scatter(1)
     each(outgoing, lambda copy: copy.start(), early, nc)
-    drain(0, True)
-    gather(1, False)
-    fill_tables([total[1, i * ng + g] for i in range(MOMENTS)], table2, factor2)
+    drain(0)
+    gather(1)
+    fill_tables([total1[i] for i in range(MOMENTS)], table2, factor2)
 
     def relax(source, s, c):
         def body(i):
@@ -372,7 +378,7 @@
 
     loop(nc, last)
     each(outgoing, lambda copy: copy.wait_send())
-    drain(1, False)
+    drain(1)
 
 
 def on_device(distribution):
@@ -394,13 +400,16 @@
             pltpu.VMEM((n, nx, cells), f32),
             pltpu.VMEM((ng, n, xs, cells), f32),
             pltpu.VMEM((COLLISIONS, MOMENTS, ng, xs, cells), f32),
-            pltpu.VMEM((COLLISIONS, nv * ng - 1, xs, cells), f32),
-            pltpu.VMEM((COLLISIONS, MOMENTS * ng, xs, cells), f32),
+            pltpu.VMEM((nv * ng - 1, ng, xs, cells), f32),
+            pltpu.VMEM((MOMENTS, ng, xs, cells), f32),
+            pltpu.VMEM((nv * ng - 1, xs, cells), f32),
+            pltpu.VMEM((MOMENTS, xs, cells), f32),
             pltpu.VMEM((3, NV1, nx, cells), f32),
             pltpu.VMEM((2, nx, cells), f32),
             pltpu.VMEM((3, NV1, xs, cells), f32),
             pltpu.VMEM((2, xs, cells), f32),
             pltpu.VMEM((4, cells, cells), jnp.bfloat16),
+            pltpu.SemaphoreType.REGULAR(((nv * ng).bit_length(),)),
             dma(()),
             dma((max(ng - 1, 1), nc)),
             dma((max(ng - 1, 1), nc)),

time: 45.6 us -> 43.7 us (0.958)
  Pallas kernels: 44.5 us -> 42.6 us
    pallas_call x1, Pallas kernels: 44.5 us -> 42.6 us  [on_device(): pl.pallas_call(functools.partial(kernel, nv, ng), out_shape=pltpu.VMEM(di...]
where the time goes in v4:
time: 43.7 us; the launch traced here: 43.6 us
  Pallas kernels  42.6 us (97%)
  local copies, waits for them, and re-layouts  0.97 us (2%)
    pallas_call x1, Pallas kernels, on_device(): pl.pallas_call(functools.partial(kernel, nv, ng), out_shape=pltpu.VMEM(di...  42.6 us
    unnamed x1, local copies, waits for them, and re-layouts  0.97 us

profile of v4, /device:TPU:0, one launch (start us, length us, event | category | flops | bytes accessed | tf_op | source)
XLA Modules:
  0.0 43.6 jit_solution(12052016079947392761)
XLA Ops:
  0.0 42.6 %shard_map.17 = f32[256,4,256]{2,1,0:T(4,128)S(1)} custom-call(f32[256,4,256]{2,1,0:T(4,128)} %src.1), custom_call_target="tpu_custom_call" | custom-call | tf_op jit(solution)/shard_map/pallas_call | solution.py:393
  42.6 1.0 %copy.3 = f32[256,4,256]{2,1,0:T(4,128)} copy(f32[256,4,256]{2,1,0:T(4,128)S(1)} %shard_map.17) | data formatting | bytes 2097152

commit v5 on v4

--- a/solution.py
+++ b/solution.py
@@ -320,7 +320,6 @@
     sums = lax.fori_loop(0, nc, first_chunk, zero)
     write_part(0, sums)
     scatter(0)
-    each(incoming, lambda copy: copy.wait_send())
     gather(0)
     fill_tables(
         [jnp.concatenate([total0[i, s] for s in range(ng)], axis=0) for i in range(MOMENTS)],
@@ -353,13 +352,16 @@
     write_part(1, sums)
     scatter(1)
     each(outgoing, lambda copy: copy.start(), early, nc)
+    each(incoming, lambda copy: copy.wait_send())
     drain(0)
     gather(1)
     fill_tables([total1[i] for i in range(MOMENTS)], table2, factor2)
 
+    group = 4 if nc % 4 == 0 else 1
+
     def relax(source, s, c):
-        def body(i):
-            j = c * size + i * NV1
+        for i in range(group * size // NV1):
+            j = c * group * size + i * NV1
             _, iy, iz = parts_of(v * count + s * n + j)
             rest = factor2[1] * table2[1, iy] * table2[2, iz]
             for ix in range(0, NV1, BLOCK):
@@ -367,16 +369,15 @@
                     factor2[0] * source[s, pl.ds(j + ix, BLOCK)] + rest * table2[0, ix : ix + BLOCK]
                 )
 
-        loop(size // NV1, body)
-
-    loop(nc, lambda c: relax(slab, g, c))
+    loop(nc // group, lambda c: relax(slab, g, c))
 
     def last(c):
         for d in range(1, ng):
-            outgoing(d, c).wait_recv()
+            for k in range(group):
+                outgoing(d, c * group + k).wait_recv()
             relax(back, lax.rem(g - d + ng, ng), c)
 
-    loop(nc, last)
+    loop(nc // group, last)
     each(outgoing, lambda copy: copy.wait_send())
     drain(1)
 

time: 43.7 us -> 43.7 us (level)
  no operation moved by 1% of the time
where the time goes in v5:
time: 43.7 us; the launch traced here: 43.6 us
  Pallas kernels  42.6 us (97%)
  local copies, waits for them, and re-layouts  0.97 us (2%)
    pallas_call x1, Pallas kernels, on_device(): pl.pallas_call(functools.partial(kernel, nv, ng), out_shape=pltpu.VMEM(di...  42.6 us
    unnamed x1, local copies, waits for them, and re-layouts  0.97 us

profile of v5, /device:TPU:0, one launch (start us, length us, event | category | flops | bytes accessed | tf_op | source)
XLA Modules:
  0.0 43.6 jit_solution(16625315208680886822)
XLA Ops:
  0.0 42.6 %shard_map.17 = f32[256,4,256]{2,1,0:T(4,128)S(1)} custom-call(f32[256,4,256]{2,1,0:T(4,128)} %src.1), custom_call_target="tpu_custom_call" | custom-call | tf_op jit(solution)/shard_map/pallas_call | solution.py:394
  42.6 1.0 %copy.3 = f32[256,4,256]{2,1,0:T(4,128)} copy(f32[256,4,256]{2,1,0:T(4,128)S(1)} %shard_map.17) | data formatting | bytes 2097152
